TPU v7x, 256 devices: a whole 4x4x8 slice. The times are simulated.
256 devices in a mesh: row: 64 (over y, z, core), col: 4 (over x).
Axes of the slice: x: 4, y: 4, z: 8, core: 2. Of those that a mesh axis runs over, the one named last changes fastest.
Arguments:
- factor: float32 [8192, 8192], P('row', 'col'), may hold values from -0.125 to 0.125
- rhs: float32 [8192, 512], P('row', 'col'), may hold values from -6 to 6
- parent: int32 [7], replicated, may hold values from 4 to 6, as said below
- bounds: int32 [8], replicated, may hold values from 0 to 64, as said below
- slot: int32 [64], replicated, may hold values from 0 to 63, each once
- structure: int32 [7, 64], replicated, may hold values 0 or 1
Outputs:
- solution: float32 [8192, 512], P('row', 'col')
Inputs may be any that keep to these rules, and one draw needn't show every extreme that they name: parent[s] is 4 or 5 for s = 0 to 3, and 6 for s = 4, 5, 6 (the root is its own entry). bounds[0] = 0, bounds[7] = 64, strictly increasing; supernode s holds logical blocks bounds[s] to bounds[s+1] - 1. `slot`: a permutation.
All inputs are finite; a program needn't handle non-finite values.
Results may differ from a plain program's by a relative error of at most 0.0001.
Values sent between devices are 32-bit elements; how exact they have to be, the bound alone decides.
A program may use at most 64 MiB of HBM per device.

v0:
```python
import jax
import jax.numpy as jnp
from jax import lax
from jax.sharding import PartitionSpec as P

B = 128
RB = 1


def block_masks(parent, bounds, slot, structure):
    count = slot.shape[0]
    ar = jnp.arange(count, dtype=jnp.int32)
    logical = jnp.sum(jnp.where(slot[:, None] == ar[None, :], ar[:, None], 0), axis=0)
    node = jnp.sum((logical[:, None] >= bounds[None, 1:7]).astype(jnp.int32), axis=1)
    level = (node >= 4).astype(jnp.int32) + (node >= 6).astype(jnp.int32)
    nodes = jnp.arange(7, dtype=jnp.int32)
    grand = parent[parent]
    ancestor = ((nodes[None, :] == parent[:, None]) | (nodes[None, :] == grand[:, None])) & (
        nodes[None, :] != nodes[:, None]
    )
    node_hot = (node[:, None] == nodes[None, :]).astype(jnp.float32)
    perm_hot = (logical[:, None] == ar[None, :]).astype(jnp.float32)
    listed_store = jnp.dot(
        structure.astype(jnp.float32), perm_hot.T, precision=lax.Precision.HIGHEST
    )
    anc_pairs = jnp.dot(
        node_hot,
        jnp.dot(ancestor.astype(jnp.float32), node_hot.T, precision=lax.Precision.HIGHEST),
        precision=lax.Precision.HIGHEST,
    )
    list_pairs = jnp.dot(node_hot, listed_store, precision=lax.Precision.HIGHEST)
    link = (anc_pairs * list_pairs).T > 0.5
    same = node[:, None] == node[None, :]
    return (level, same, link)


def masked(block_rows, mask):
    rblocks, width = mask.shape
    bsz = block_rows.shape[0] // rblocks
    shaped = block_rows.reshape(rblocks, bsz, width, bsz) * mask[:, None, :, None].astype(
        jnp.float32
    )
    return shaped.reshape(block_rows.shape)


def body(factor, rhs, parent, bounds, slot, structure):
    level, same, link = block_masks(parent, bounds, slot, structure)
    first = lax.axis_index("row") * RB
    level_mine = lax.dynamic_slice_in_dim(level, first, RB, 0)
    same_mine = lax.dynamic_slice_in_dim(same, first, RB, 0)
    link_mine = lax.dynamic_slice_in_dim(link, first, RB, 0)
    full_rows = lax.all_gather(factor, "col", axis=1, tiled=True)
    diag_part = masked(full_rows, same_mine)
    link_part = masked(full_rows, link_mine)

    def product(matrix, vector):
        return jnp.dot(
            matrix,
            lax.all_gather(vector, "row", axis=0, tiled=True),
            precision=lax.Precision.HIGHEST,
            preferred_element_type=jnp.float32,
        )

    pieces = [rhs]
    accums = [jnp.zeros(p.shape, jnp.float32) for p in pieces]
    results = [jnp.zeros(p.shape, jnp.float32) for p in pieces]
    for section in range(3):
        rows = jnp.repeat(level_mine == section, B)[:, None]
        solved = jnp.where(rows, product(diag_part, pieces[0] - accums[0]), 0.0)
        results[0] = results[0] + solved
        if section < 2:
            accums[0] = accums[0] + product(link_part, solved)
    return results[0]


def solution(mesh):
    in_specs = (P("row", "col"), P("row", "col"), P(), P(), P(), P())
    out_specs = P("row", "col")
    return jax.shard_map(body, mesh=mesh, in_specs=in_specs, out_specs=out_specs, check_vma=False)
```

profile of v0, /device:TPU:1, one launch (start us, length us, event | category | flops | bytes accessed | tf_op | source)
XLA Modules:
  0.0 501.4 jit_solution(158808282834339269)
XLA Ops:
  6.5 0.7 all-gather.7.cloned.1.call-update
  7.3 0.7 all-gather.9.cloned.1.call-update
  8.1 0.7 slice.3
  8.8 0.7 select_reduce_fusion
  9.6 0.6 dynamic-slice
  10.2 0.7 dynamic_slice.9
  11.6 0.7 fusion.48
  12.3 51.4 %all-gather.7.cloned.1.call-done = f32[128,8192]{1,0:T(8,128)} async-done(((f32[128,2048]{1,0:T(8,128)}), f32[128,8192]{1,0:T(8,128)}) %all-gather.7.cloned.1.call-update) | async-done | bytes 4194320 | tf_op jit(solution)/shard_map/all_gather | solution.py:52
  63.8 82.7 %all-gather.9.cloned.1.call-done = f32[8192,128]{1,0:T(8,128)} async-done(((f32[128,128]{1,0:T(8,128)}), f32[8192,128]{1,0:T(8,128)}) %all-gather.9.cloned.1.call-update) | async-done | bytes 4194320 | tf_op jit(solution)/shard_map/all_gather | solution.py:59
  146.5 8.4 %fusion.15 = f32[128,128]{1,0:T(8,128)} fusion(f32[8192,128]{1,0:T(8,128)} %all-gather.9.cloned.1.call-done, f32[128,8192]{1,0:T(8,128)} %all-gather.7.cloned.1.call-done, f32[8192]{0:T(1024)S(1)} %broadcast_bitcast_fusion.1, pred[]{:T(512)} %bitcast), kind=kOutput, calls=%fused_computation.16 | convolution fusion | flops 1611677696 | bytes 8486913 | tf_op jit(solution)/shard_map/dot_general | solution.py:57
  155.0 0.6 gather_fusion
  155.6 0.2 fusion.35
  155.8 0.2 fusion.36
  156.0 0.3 fusion.33
  156.3 0.2 fusion.34
  156.7 74.7 %all-gather.11.cloned.1.call-done = f32[8192,128]{1,0:T(8,128)} async-done(((f32[128,128]{1,0:T(8,128)}), f32[8192,128]{1,0:T(8,128)}) %all-gather.11.cloned.1.call-update) | async-done | bytes 4194320 | tf_op jit(solution)/shard_map/all_gather | solution.py:59
  231.4 8.4 %fusion.50 = (f32[128,128]{1,0:T(8,128)}, f32[128,128]{1,0:T(8,128)S(1)}) fusion(f32[128,128]{1,0:T(8,128)S(1)} %copy-done.1, f32[8192,128]{1,0:T(8,128)} %all-gather.11.cloned.1.call-done, f32[128,8192]{1,0:T(8,128)} %all-gather.7.cloned.1.call-done, f32[8192]{0:T(1024)S(1)} %broadcast_bitcast_fusion), kind=kOutput, calls=%fused_computation.55 | convolution fusion | flops 1611677696 | bytes 8617984 | tf_op jit(solution)/shard_map/dot_general | solution.py:57
  239.8 0.2 all-gather.15.cloned.1.call-start
  240.7 75.6 %all-gather.13.cloned.1.call-done = f32[8192,128]{1,0:T(8,128)} async-done(((f32[128,128]{1,0:T(8,128)}), f32[8192,128]{1,0:T(8,128)}) %all-gather.13.cloned.1.call-update) | async-done | bytes 4194320 | tf_op jit(solution)/shard_map/all_gather | solution.py:59
  316.3 8.4 %fusion.18 = f32[128,128]{1,0:T(8,128)} fusion(f32[8192,128]{1,0:T(8,128)} %all-gather.13.cloned.1.call-done, f32[128,8192]{1,0:T(8,128)} %all-gather.7.cloned.1.call-done, f32[8192]{0:T(1024)S(1)} %broadcast_bitcast_fusion.1, pred[]{:T(512)} %bitcast.3), kind=kOutput, calls=%fused_computation.17 | convolution fusion | flops 1611677696 | bytes 8486913 | tf_op jit(solution)/shard_map/dot_general | solution.py:57
  324.8 76.4 %all-gather.15.cloned.1.call-done = f32[8192,128]{1,0:T(8,128)} async-done(((f32[128,128]{1,0:T(8,128)}), f32[8192,128]{1,0:T(8,128)}) %all-gather.15.cloned.1.call-update) | async-done | bytes 4194320 | tf_op jit(solution)/shard_map/all_gather | solution.py:59
  401.2 8.4 %fusion.30 = f32[128,128]{1,0:T(8,128)} fusion(f32[128,128]{1,0:T(8,128)S(1)} %copy-done.1, f32[128,128]{1,0:T(8,128)S(1)} %get-tuple-element.6, f32[8192,128]{1,0:T(8,128)} %all-gather.15.cloned.1.call-done, f32[128,8192]{1,0:T(8,128)} %all-gather.7.cloned.1.call-done, f32[8192]{0:T(1024)S(1)} %broadcast_bitcast_fusion), kind=kOutput, calls=%fused_computation.21 | convolution fusion | flops 1611694080 | bytes 8617984 | tf_op jit(solution)/shard_map/dot_general | solution.py:57
  410.3 75.8 %all-gather.17.cloned.1.call-done = f32[8192,128]{1,0:T(8,128)} async-done(((f32[128,128]{1,0:T(8,128)}), f32[8192,128]{1,0:T(8,128)}) %all-gather.17.cloned.1.call-update) | async-done | bytes 4194320 | tf_op jit(solution)/shard_map/all_gather | solution.py:59
  486.1 8.4 %fusion.24 = f32[128,128]{1,0:T(8,128)} fusion(f32[8192,128]{1,0:T(8,128)} %all-gather.17.cloned.1.call-done, f32[128,8192]{1,0:T(8,128)} %all-gather.7.cloned.1.call-done, f32[8192]{0:T(1024)S(1)} %broadcast_bitcast_fusion.1, f32[128,128]{1,0:T(8,128)S(1)} %copy-done.2, f32[128,128]{1,0:T(8,128)S(1)} %copy-done.3, pred[]{:T(512)} %bitcast.6), kind=kOutput, calls=%fused_computation.19 | convolution fusion | flops 1611710464 | bytes 8617985 | tf_op jit(solution)/shard_map/dot_general | solution.py:57
  (26 shorter events, 0.5 us)
Async XLA Ops:
  6.5 57.2 %all-gather.7.cloned.1.call-start = ((), (), s32[]{:S(2)}) async-start(), calls=%async_computation | async-start | bytes 5242880 | tf_op jit(solution)/shard_map/all_gather | solution.py:52
  7.3 139.2 %all-gather.9.cloned.1.call-start = ((), (), s32[]{:S(2)}) async-start(), calls=%async_computation.1 | async-start | bytes 4259840 | tf_op jit(solution)/shard_map/all_gather | solution.py:59
  8.0 223.4 %all-gather.11.cloned.1.call-start = ((), (), s32[]{:S(2)}) async-start(), calls=%async_computation.2 | async-start | bytes 4259840 | tf_op jit(solution)/shard_map/all_gather | solution.py:59
  146.5 8.5 %copy-start = (s32[7]{0:T(128)S(1)}, s32[7]{0:T(128)}, u32[]{:S(2)}) copy-start(s32[7]{0:T(128)} %param.8) | copy-start | bytes 88
  146.5 9.4 %copy-start.4 = (s32[7,64]{1,0:T(8,128)S(1)}, s32[7,64]{1,0:T(8,128)}, u32[]{:S(2)}) copy-start(s32[7,64]{1,0:T(8,128)} %param.11) | copy-start | bytes 5380
  146.5 84.9 %copy-start.1 = (f32[128,128]{1,0:T(8,128)S(1)}, f32[128,128]{1,0:T(8,128)}, u32[]{:S(2)}) copy-start(f32[128,128]{1,0:T(8,128)} %param.7) | copy-start | bytes 196612
  154.9 161.4 %all-gather.13.cloned.1.call-start = ((), (), s32[]{:S(2)}) async-start(), calls=%async_computation.3 | async-start | bytes 4259840 | tf_op jit(solution)/shard_map/all_gather | solution.py:59
  239.8 161.4 %all-gather.15.cloned.1.call-start = ((), (), s32[]{:S(2)}) async-start(), calls=%async_computation.4 | async-start | bytes 4259840 | tf_op jit(solution)/shard_map/all_gather | solution.py:59
  324.7 161.4 %all-gather.17.cloned.1.call-start = ((), (), s32[]{:S(2)}) async-start(), calls=%async_computation.5 | async-start | bytes 4259840 | tf_op jit(solution)/shard_map/all_gather | solution.py:59
  401.2 84.9 %copy-start.2 = (f32[128,128]{1,0:T(8,128)S(1)}, f32[128,128]{1,0:T(8,128)}, u32[]{:S(2)}) copy-start(f32[128,128]{1,0:T(8,128)} %fusion.15) | copy-start | bytes 196612
  401.2 84.9 %copy-start.3 = (f32[128,128]{1,0:T(8,128)S(1)}, f32[128,128]{1,0:T(8,128)}, u32[]{:S(2)}) copy-start(f32[128,128]{1,0:T(8,128)} %fusion.18) | copy-start | bytes 196612
Sparse Core Ops, SparseCore 0:
  9.2 54.5 all-gather.6
  66.5 79.8 all-gather.8
  155.0 76.3 all-gather.10
  239.9 76.3 all-gather.12
  324.8 76.3 all-gather.14
  409.8 76.3 all-gather.16
where the time goes:
time: 501 us
  waiting for transfers between devices  438 us (87%)
  matrix products  42.9 us (9%)
  between operations  15.6 us (3%)
    all_gather x5, waiting for transfers between devices, product(): lax.all_gather(vector, 'row', axis=0, tiled=True)  385 us
    all_gather x1, waiting for transfers between devices, body(): full_rows = lax.all_gather(factor, 'col', axis=1, tiled=True)  51.4 us
    dot_general x5, matrix products, product(): jnp.dot(matrix, lax.all_gather(vector, 'row', axis=0, tiled=True), precis...  42 us
  transfers between devices with their start and end apart: 6, of which 6 were waited for; matrix products, arithmetic and copies ran while one was open for 1% of the time, Pallas kernels for 0%

commit v1 on v0

--- a/solution.py
+++ b/solution.py
@@ -5,6 +5,22 @@
 
 B = 128
 RB = 1
+
+
+def collect(x, axis, dim):
+    ways, here, turn = (lax.axis_size(axis), lax.axis_index(axis), x.shape[dim])
+    shape = [n * ways if d == dim else n for d, n in enumerate(x.shape)]
+    full = lax.dynamic_update_slice_in_dim(jnp.zeros(shape, x.dtype), x, here * turn, axis=dim)
+    going_up = going_down = x
+    for far in range(1, ways // 2 + 1):
+        going_up = lax.ppermute(going_up, axis, [(d, (d + 1) % ways) for d in range(ways)])
+        full = lax.dynamic_update_slice_in_dim(full, going_up, (here - far) % ways * turn, axis=dim)
+        if 2 * far < ways:
+            going_down = lax.ppermute(going_down, axis, [(d, (d - 1) % ways) for d in range(ways)])
+            full = lax.dynamic_update_slice_in_dim(
+                full, going_down, (here + far) % ways * turn, axis=dim
+            )
+    return full
 
 
 def block_masks(parent, bounds, slot, structure):
@@ -49,7 +65,7 @@
     level_mine = lax.dynamic_slice_in_dim(level, first, RB, 0)
     same_mine = lax.dynamic_slice_in_dim(same, first, RB, 0)
     link_mine = lax.dynamic_slice_in_dim(link, first, RB, 0)
-    full_rows = lax.all_gather(factor, "col", axis=1, tiled=True)
+    full_rows = collect(factor, "col", 1)
     diag_part = masked(full_rows, same_mine)
     link_part = masked(full_rows, link_mine)
 

time: 501 us -> 448 us (0.89)
  waiting for transfers between devices: 438 us -> 372 us
  local copies, waits for them, and re-layouts: 2.79 us -> 10.7 us
  starting transfers between devices: 0.38 us -> 5.93 us
    all_gather x1 -> x0, waiting for transfers between devices: 51.4 us -> none  [body(): full_rows = lax.all_gather(factor, 'col', axis=1, tiled=True)]
    all_gather x5, waiting for transfers between devices: 385 us -> 338 us  [product(): lax.all_gather(vector, 'row', axis=0, tiled=True)]
    ppermute x0 -> x3, waiting for transfers between devices: none -> 32.9 us  [the longest x2 32.9 us: collect(): lax.ppermute(going_up, axis, [(d, (d + 1) % ways) for d in range(ways)])]
    dynamic_update_slice x0 -> x4, local copies, waits for them, and re-layouts: none -> 5.49 us  [the longest x2 3.4 us: collect(): lax.dynamic_update_slice_in_dim(full, going_up, (here - far) % ways * tur...]
    ppermute x0 -> x3, starting transfers between devices: none -> 5.36 us  [the longest x2 4.01 us: collect(): lax.ppermute(going_up, axis, [(d, (d + 1) % ways) for d in range(ways)])]
  transfers between devices with their start and end apart: 6 -> 8, of which waited for: 6 -> 7; matrix products, arithmetic and copies ran while one was open for 1% -> 3% of each run, Pallas kernels for 0% -> 0%
where the time goes in v1:
time: 448 us
  waiting for transfers between devices  372 us (83%)
  matrix products  42.9 us (10%)
  between operations  15.3 us (3%)
  local copies, waits for them, and re-layouts  10.7 us (2%)
  starting transfers between devices  5.93 us (1%)
    all_gather x5, waiting for transfers between devices, product(): lax.all_gather(vector, 'row', axis=0, tiled=True)  338 us
    dot_general x5, matrix products, product(): jnp.dot(matrix, lax.all_gather(vector, 'row', axis=0, tiled=True), precis...  42 us
    ppermute x2, waiting for transfers between devices, collect(): lax.ppermute(going_up, axis, [(d, (d + 1) % ways) for d in range(ways)])  32.9 us
  transfers between devices with their start and end apart: 8, of which 7 were waited for; matrix products, arithmetic and copies ran while one was open for 3% of the time, Pallas kernels for 0%

profile of v1, /device:TPU:1, one launch (start us, length us, event | category | flops | bytes accessed | tf_op | source)
XLA Modules:
  0.0 448.0 jit_solution(2574681358208293760)
XLA Ops:
  6.5 0.7 all-gather.6.cloned.1.call-update
  7.3 2.1 collective-permute-start
  9.4 1.4 collective-permute-start.1
  10.8 0.7 slice.3
  11.5 0.7 select_reduce_fusion
  12.9 18.6 %collective-permute-done = f32[128,2048]{1,0:T(8,128)S(1)} collective-permute-done((f32[128,2048]{1,0:T(8,128)}, f32[128,2048]{1,0:T(8,128)S(1)}, u32[]{:S(2)}, u32[]{:S(2)}) %collective-permute-start) | collective-permute-done | bytes 1048608 | tf_op jit(solution)/shard_map/ppermute | solution.py:16
  31.5 1.9 collective-permute-start.2
  34.1 0.7 dynamic_slice.9
  35.5 2.4 broadcast_in_dim.67
  38.0 1.1 constant_dynamic-update-slice_fusion.3
  39.0 1.1 constant_dynamic-update-slice_fusion.2
  40.1 1.0 constant_dynamic-update-slice_fusion.1
  41.1 14.4 %collective-permute-done.2 = f32[128,2048]{1,0:T(8,128)} collective-permute-done((f32[128,2048]{1,0:T(8,128)S(1)}, f32[128,2048]{1,0:T(8,128)}, u32[]{:S(2)}, u32[]{:S(2)}) %collective-permute-start.2) | collective-permute-done | bytes 1048608 | tf_op jit(solution)/shard_map/ppermute | solution.py:16
  55.5 2.3 constant_dynamic-update-slice_fusion
  57.8 35.6 %all-gather.6.cloned.1.call-done = f32[8192,128]{1,0:T(8,128)} async-done(((f32[128,128]{1,0:T(8,128)}), f32[8192,128]{1,0:T(8,128)}) %all-gather.6.cloned.1.call-update) | async-done | bytes 4194320 | tf_op jit(solution)/shard_map/all_gather | solution.py:75
  93.4 8.4 %fusion.15 = f32[128,128]{1,0:T(8,128)} fusion(f32[8192,128]{1,0:T(8,128)} %all-gather.6.cloned.1.call-done, f32[128,8192]{1,0:T(8,128)} %constant_dynamic-update-slice_fusion, f32[8192]{0:T(1024)S(1)} %broadcast_bitcast_fusion.1, pred[]{:T(512)} %bitcast), kind=kOutput, calls=%fused_computation.16 | convolution fusion | flops 1611677696 | bytes 8486913 | tf_op jit(solution)/shard_map/dot_general | solution.py:73
  103.8 74.6 %all-gather.8.cloned.1.call-done = f32[8192,128]{1,0:T(8,128)} async-done(((f32[128,128]{1,0:T(8,128)}), f32[8192,128]{1,0:T(8,128)}) %all-gather.8.cloned.1.call-update) | async-done | bytes 4194320 | tf_op jit(solution)/shard_map/all_gather | solution.py:75
  178.4 8.4 %fusion.50 = (f32[128,128]{1,0:T(8,128)}, f32[128,128]{1,0:T(8,128)S(1)}) fusion(f32[128,128]{1,0:T(8,128)S(1)} %copy-done.2, f32[8192,128]{1,0:T(8,128)} %all-gather.8.cloned.1.call-done, f32[128,8192]{1,0:T(8,128)} %constant_dynamic-update-slice_fusion, f32[8192]{0:T(1024)S(1)} %broadcast_bitcast_fusion), kind=kOutput, calls=%fused_computation.61 | convolution fusion | flops 1611677696 | bytes 8617984 | tf_op jit(solution)/shard_map/dot_general | solution.py:73
  187.5 75.7 %all-gather.10.cloned.1.call-done = f32[8192,128]{1,0:T(8,128)} async-done(((f32[128,128]{1,0:T(8,128)}), f32[8192,128]{1,0:T(8,128)}) %all-gather.10.cloned.1.call-update) | async-done | bytes 4194320 | tf_op jit(solution)/shard_map/all_gather | solution.py:75
  263.3 8.4 %fusion.18 = f32[128,128]{1,0:T(8,128)} fusion(f32[8192,128]{1,0:T(8,128)} %all-gather.10.cloned.1.call-done, f32[128,8192]{1,0:T(8,128)} %constant_dynamic-update-slice_fusion, f32[8192]{0:T(1024)S(1)} %broadcast_bitcast_fusion.1, pred[]{:T(512)} %bitcast.3), kind=kOutput, calls=%fused_computation.17 | convolution fusion | flops 1611677696 | bytes 8486913 | tf_op jit(solution)/shard_map/dot_general | solution.py:73
  271.9 76.2 %all-gather.12.cloned.1.call-done = f32[8192,128]{1,0:T(8,128)} async-done(((f32[128,128]{1,0:T(8,128)}), f32[8192,128]{1,0:T(8,128)}) %all-gather.12.cloned.1.call-update) | async-done | bytes 4194320 | tf_op jit(solution)/shard_map/all_gather | solution.py:75
  348.1 8.4 %fusion.27 = f32[128,128]{1,0:T(8,128)} fusion(f32[128,128]{1,0:T(8,128)S(1)} %copy-done.2, f32[128,128]{1,0:T(8,128)S(1)} %get-tuple-element.6, f32[8192,128]{1,0:T(8,128)} %all-gather.12.cloned.1.call-done, f32[128,8192]{1,0:T(8,128)} %constant_dynamic-update-slice_fusion, f32[8192]{0:T(1024)S(1)} %broadcast_bitcast_fusion), kind=kOutput, calls=%fused_computation.20 | convolution fusion | flops 1611694080 | bytes 8617984 | tf_op jit(solution)/shard_map/dot_general | solution.py:73
  357.3 75.8 %all-gather.14.cloned.1.call-done = f32[8192,128]{1,0:T(8,128)} async-done(((f32[128,128]{1,0:T(8,128)}), f32[8192,128]{1,0:T(8,128)}) %all-gather.14.cloned.1.call-update) | async-done | bytes 4194320 | tf_op jit(solution)/shard_map/all_gather | solution.py:75
  433.1 8.4 %add_add_fusion = f32[128,128]{1,0:T(8,128)} fusion(f32[128,128]{1,0:T(8,128)S(1)} %copy-done.3, f32[128,128]{1,0:T(8,128)S(1)} %copy-done.4, f32[8192,128]{1,0:T(8,128)} %all-gather.14.cloned.1.call-done, f32[128,8192]{1,0:T(8,128)} %constant_dynamic-update-slice_fusion, f32[8192]{0:T(1024)S(1)} %broadcast_bitcast_fusion.1, pred[]{:T(512)} %bitcast.6), kind=kOutput, calls=%fused_computation.21 | convolution fusion | flops 1611710464 | bytes 8617985 | tf_op jit(solution)/shard_map/dot_general | solution.py:73
  (36 shorter events, 3.7 us)
Async XLA Ops:
  6.5 31.4 %copy-start.1 = (f32[128,2048]{1,0:T(8,128)S(1)}, f32[128,2048]{1,0:T(8,128)}, u32[]{:S(2)}) copy-start(f32[128,2048]{1,0:T(8,128)} %param.6) | copy-start | bytes 3145732
  6.5 86.9 %all-gather.6.cloned.1.call-start = ((), (), s32[]{:S(2)}) async-start(), calls=%async_computation | async-start | bytes 4259840 | tf_op jit(solution)/shard_map/all_gather | solution.py:75
  7.3 171.1 %all-gather.8.cloned.1.call-start = ((), (), s32[]{:S(2)}) async-start(), calls=%async_computation.1 | async-start | bytes 4259840 | tf_op jit(solution)/shard_map/all_gather | solution.py:75
  7.3 24.2 %collective-permute-start = (f32[128,2048]{1,0:T(8,128)}, f32[128,2048]{1,0:T(8,128)S(1)}, u32[]{:S(2)}, u32[]{:S(2)}) collective-permute-start(f32[128,2048]{1,0:T(8,128)} %param.6), channel_id=1, source_target_pairs={{0,1},{1,2},{2,3},{3,0},{4,5},{5,6},{6,7},{7,4},{8,9},{9,10},{10,1... | collective-permute-start | bytes 3145736 | tf_op jit(solution)/shard_map/ppermute | solution.py:16
  9.4 30.7 %collective-permute-start.1 = (f32[128,2048]{1,0:T(8,128)}, f32[128,2048]{1,0:T(8,128)S(1)}, u32[]{:S(2)}, u32[]{:S(2)}) collective-permute-start(f32[128,2048]{1,0:T(8,128)} %param.6), channel_id=1, source_target_pairs={{0,3},{1,0},{2,1},{3,2},{4,7},{5,4},{6,5},{7,6},{8,11},{9,8},{10,9... | collective-permute-start | bytes 3145736 | tf_op jit(solution)/shard_map/ppermute | solution.py:19
  31.5 24.0 %collective-permute-start.2 = (f32[128,2048]{1,0:T(8,128)S(1)}, f32[128,2048]{1,0:T(8,128)}, u32[]{:S(2)}, u32[]{:S(2)}) collective-permute-start(f32[128,2048]{1,0:T(8,128)S(1)} %collective-permute-done), channel_id=1, source_target_pairs={{0,1},{1,2},{2,3},{3,0},{4,5},{5,6},{6,7},{7,4},{8,9},{9,10},{10,1... | collective-permute-start | bytes 3145736 | tf_op jit(solution)/shard_map/ppermute | solution.py:16
  93.4 8.7 %copy-start = (s32[7]{0:T(128)S(1)}, s32[7]{0:T(128)}, u32[]{:S(2)}) copy-start(s32[7]{0:T(128)} %param.8) | copy-start | bytes 88
  93.4 9.6 %copy-start.5 = (s32[7,64]{1,0:T(8,128)S(1)}, s32[7,64]{1,0:T(8,128)}, u32[]{:S(2)}) copy-start(s32[7,64]{1,0:T(8,128)} %param.11) | copy-start | bytes 5380
  93.4 84.9 %copy-start.2 = (f32[128,128]{1,0:T(8,128)S(1)}, f32[128,128]{1,0:T(8,128)}, u32[]{:S(2)}) copy-start(f32[128,128]{1,0:T(8,128)} %param.7) | copy-start | bytes 196612
  101.9 161.4 %all-gather.10.cloned.1.call-start = ((), (), s32[]{:S(2)}) async-start(), calls=%async_computation.2 | async-start | bytes 4259840 | tf_op jit(solution)/shard_map/all_gather | solution.py:75
  186.8 161.4 %all-gather.12.cloned.1.call-start = ((), (), s32[]{:S(2)}) async-start(), calls=%async_computation.3 | async-start | bytes 4259840 | tf_op jit(solution)/shard_map/all_gather | solution.py:75
  271.7 161.4 %all-gather.14.cloned.1.call-start = ((), (), s32[]{:S(2)}) async-start(), calls=%async_computation.4 | async-start | bytes 4259840 | tf_op jit(solution)/shard_map/all_gather | solution.py:75
  348.1 84.9 %copy-start.3 = (f32[128,128]{1,0:T(8,128)S(1)}, f32[128,128]{1,0:T(8,128)}, u32[]{:S(2)}) copy-start(f32[128,128]{1,0:T(8,128)} %fusion.15) | copy-start | bytes 196612
  348.1 84.9 %copy-start.4 = (f32[128,128]{1,0:T(8,128)S(1)}, f32[128,128]{1,0:T(8,128)}, u32[]{:S(2)}) copy-start(f32[128,128]{1,0:T(8,128)} %fusion.18) | copy-start | bytes 196612
Sparse Core Ops, SparseCore 0:
  10.1 83.2 all-gather.5
  102.0 76.3 all-gather.7
  186.9 76.3 all-gather.9
  271.8 76.3 all-gather.11
  356.7 76.3 all-gather.13
